TPU v7x, 32 devices: a whole 2x2x4 slice. The times are simulated.
32 devices in a mesh: dp: 8 (over z, x), mp: 4 (over y, core).
Axes of the slice: x: 2, y: 2, z: 4, core: 2. Of those that a mesh axis runs over, the one named last changes fastest.
Arguments:
- hidden_in: bfloat16 [8, 2048, 960], P('dp', 'mp'), may hold values from -6 to 6
- cotangent: bfloat16 [8, 2048, 960], P('dp', 'mp'), may hold values from -6 to 6
- segments: int32 [8, 2048], P('dp'), may hold values from 0 to 3, never falling along the last dimension, each value on 1 to 1024 neighbouring positions
- positions: int32 [8, 2048], P('dp', 'mp'), may hold values from 0 to 4095
- attn_in: bfloat16 [960, 1600], P('dp', 'mp'), may hold values from -0.1875 to 0.1875
- attn_out: bfloat16 [960, 960], P('mp', 'dp'), may hold values from -0.75 to 0.75
- w_gate: bfloat16 [960, 2560], P('dp', 'mp'), may hold values from -0.1875 to 0.1875
- w_up: bfloat16 [960, 2560], P('dp', 'mp'), may hold values from -0.1875 to 0.1875
- w_down: bfloat16 [2560, 960], P('mp', 'dp'), may hold values from -0.125 to 0.125
- norm1_gain: bfloat16 [960], P('dp'), may hold values from 0.099609375 to 1.8984375
- norm2_gain: bfloat16 [960], P('dp'), may hold values from 0.099609375 to 1.8984375
Outputs:
- hidden_out: bfloat16 [8, 2048, 960], P('dp', 'mp')
- grad_hidden: float32 [8, 2048, 960], P('dp', 'mp')
- grad_attn_in: float32 [960, 1600], P('dp', 'mp')
- grad_attn_out: float32 [960, 960], P('mp', 'dp')
- grad_gate: float32 [960, 2560], P('dp', 'mp')
- grad_up: float32 [960, 2560], P('dp', 'mp')
- grad_down: float32 [2560, 960], P('mp', 'dp')
- grad_gain1: float32 [960], P('dp')
- grad_gain2: float32 [960], P('dp')
Inputs may be any that keep to these rules, and one draw needn't show every extreme that they name: `segments`: segment numbers never fall along a sequence; every segment is a run of 1 to 1024 tokens.
All inputs are finite; a program needn't handle non-finite values.
Results may differ from a plain program's by a relative error of at most 0.015.
Values may be sent and summed in bfloat16 or wider, within the bound.
A program may use at most 192 MiB of HBM per device.

v0:
```python
import math
import jax
import jax.numpy as jnp
from jax import lax
from jax.sharding import PartitionSpec as P

HEADS = 15
KV_HEADS = 5
HEAD_DIM = 64
EPSILON = 1e-05
SCORE_SCALE = 0.125
MASK_FILL = -1e30


def rms_forward(values_in, gain):
    inverse = lax.rsqrt(jnp.mean(values_in * values_in, axis=-1, keepdims=True) + EPSILON)
    return (values_in * inverse * gain, inverse)


def rms_backward(values_in, inverse, gain, upstream):
    scaled = upstream * gain
    grad_in = inverse * (
        scaled
        - values_in * inverse * inverse * jnp.mean(scaled * values_in, axis=-1, keepdims=True)
    )
    return (grad_in, jnp.sum(upstream * values_in * inverse, axis=0))


def rotary_tables(position_ids):
    half_dim = HEAD_DIM // 2
    frequency = jnp.exp(
        jnp.arange(half_dim, dtype=jnp.float32) * (-2.0 * math.log(10000.0) / HEAD_DIM)
    )
    angles = position_ids.astype(jnp.float32)[:, None] * frequency[None, :]
    return (jnp.cos(angles)[:, None, :], jnp.sin(angles)[:, None, :])


def rotate(tensor, cosine, sine):
    half_dim = HEAD_DIM // 2
    first, second = (tensor[..., :half_dim], tensor[..., half_dim:])
    return jnp.concatenate(
        [first * cosine - second * sine, second * cosine + first * sine], axis=-1
    )


def rotate_back(tensor, cosine, sine):
    half_dim = HEAD_DIM // 2
    first, second = (tensor[..., :half_dim], tensor[..., half_dim:])
    return jnp.concatenate(
        [first * cosine + second * sine, second * cosine - first * sine], axis=-1
    )


def score_block(queries, keys, allowed):
    scores = (
        jnp.einsum("grd,sd->grs", queries, keys, preferred_element_type=jnp.float32) * SCORE_SCALE
    )
    return jnp.where(allowed[None], scores, MASK_FILL)


def attend(queries, keys, values, allowed):
    scores = score_block(queries, keys, allowed)
    peak = jnp.max(scores, axis=-1, keepdims=True)
    total = jnp.sum(jnp.exp(scores - peak), axis=-1, keepdims=True)
    log_total = peak + jnp.log(total)
    probs = jnp.exp(scores - log_total).astype(jnp.bfloat16)
    output = jnp.einsum("grs,sd->grd", probs, values, preferred_element_type=jnp.float32)
    return (output, log_total[..., 0])


def attend_back(queries, keys, values, allowed, log_total, output_b, grad_out_b):
    scores = score_block(queries, keys, allowed)
    probs = jnp.exp(scores - log_total[..., None])
    probs_b = probs.astype(jnp.bfloat16)
    grad_probs = jnp.einsum("grd,sd->grs", grad_out_b, values, preferred_element_type=jnp.float32)
    delta = jnp.sum(
        grad_out_b.astype(jnp.float32) * output_b.astype(jnp.float32), axis=-1, keepdims=True
    )
    grad_scores = (probs * (grad_probs - delta)).astype(jnp.bfloat16)
    grad_q = (
        jnp.einsum("grs,sd->grd", grad_scores, keys, preferred_element_type=jnp.float32)
        * SCORE_SCALE
    )
    grad_k = (
        jnp.einsum("grs,grd->sd", grad_scores, queries, preferred_element_type=jnp.float32)
        * SCORE_SCALE
    )
    grad_v = jnp.einsum("grs,grd->sd", probs_b, grad_out_b, preferred_element_type=jnp.float32)
    return (grad_q, grad_k, grad_v)


def per_device(
    hidden_in,
    cotangent,
    segments,
    positions,
    attn_in,
    attn_out,
    w_gate,
    w_up,
    w_down,
    norm1_gain,
    norm2_gain,
):
    tok_rows = hidden_in.shape[1]
    model_size = lax.axis_size("mp")
    seq_rows = tok_rows * model_size
    model_rank = lax.axis_index("mp")
    group_size = HEADS // KV_HEADS
    query_cols = HEADS * HEAD_DIM
    kv_cols = KV_HEADS * HEAD_DIM
    gathered = (
        lax.all_gather(attn_in, "dp", axis=0, tiled=True),
        lax.all_gather(attn_out, "dp", axis=1, tiled=True),
        lax.all_gather(w_gate, "dp", axis=0, tiled=True),
        lax.all_gather(w_up, "dp", axis=0, tiled=True),
        lax.all_gather(w_down, "dp", axis=1, tiled=True),
        lax.all_gather(norm1_gain, "dp", axis=0, tiled=True),
        lax.all_gather(norm2_gain, "dp", axis=0, tiled=True),
    )
    qkv_weight, out_weight = (
        lax.all_gather(gathered[0], "mp", axis=1, tiled=True),
        lax.all_gather(gathered[1], "mp", axis=0, tiled=True),
    )
    gate_weight, up_weight, down_weight = (gathered[2], gathered[3], gathered[4])
    gain_one = gathered[5].astype(jnp.float32)
    gain_two = gathered[6].astype(jnp.float32)
    resid_in = hidden_in[0].astype(jnp.float32)
    normed1, inv_one = rms_forward(resid_in, gain_one)
    normed1_b = normed1.astype(jnp.bfloat16)
    projected = jnp.dot(normed1_b, qkv_weight, preferred_element_type=jnp.float32)
    cosine, sine = rotary_tables(positions[0])
    queries = rotate(
        projected[:, :query_cols].reshape(tok_rows, HEADS, HEAD_DIM), cosine, sine
    ).astype(jnp.bfloat16)
    keys_own = (
        rotate(
            projected[:, query_cols : query_cols + kv_cols].reshape(tok_rows, KV_HEADS, HEAD_DIM),
            cosine,
            sine,
        )
        .astype(jnp.bfloat16)
        .reshape(tok_rows, kv_cols)
    )
    values_own = projected[:, query_cols + kv_cols :].astype(jnp.bfloat16)
    keys_all, values_all = (
        lax.all_gather(keys_own, "mp", axis=0, tiled=True),
        lax.all_gather(values_own, "mp", axis=0, tiled=True),
    )
    seq_seg = segments[0]
    query_seg = lax.dynamic_slice_in_dim(seq_seg, model_rank * tok_rows, tok_rows, 0)
    query_index = model_rank * tok_rows + jnp.arange(tok_rows, dtype=jnp.int32)
    key_index = jnp.arange(seq_rows, dtype=jnp.int32)
    allowed = (query_seg[:, None] == seq_seg[None, :]) & (
        key_index[None, :] <= query_index[:, None]
    )
    query_groups = queries.reshape(tok_rows, KV_HEADS, group_size, HEAD_DIM).transpose(1, 2, 0, 3)
    key_groups = keys_all.reshape(seq_rows, KV_HEADS, HEAD_DIM).transpose(1, 0, 2)
    value_groups = values_all.reshape(seq_rows, KV_HEADS, HEAD_DIM).transpose(1, 0, 2)
    outputs, log_totals = lax.map(
        lambda pack: attend(pack[0], pack[1], pack[2], allowed),
        (query_groups, key_groups, value_groups),
    )
    out_groups = outputs.astype(jnp.bfloat16)
    attn_b = out_groups.transpose(2, 0, 1, 3).reshape(tok_rows, query_cols)
    middle = resid_in + jnp.dot(attn_b, out_weight, preferred_element_type=jnp.float32)
    normed2, inv_two = rms_forward(middle, gain_two)
    normed2_b = normed2.astype(jnp.bfloat16)
    seq_normed = lax.all_gather(normed2_b, "mp", axis=0, tiled=True)
    gate = jnp.dot(seq_normed, gate_weight, preferred_element_type=jnp.float32)
    upper = jnp.dot(seq_normed, up_weight, preferred_element_type=jnp.float32)
    sigma = jax.nn.sigmoid(gate)
    silu_gate = gate * sigma
    hidden_b = (silu_gate * upper).astype(jnp.bfloat16)
    ffn_out = lax.psum_scatter(
        jnp.dot(hidden_b, down_weight, preferred_element_type=jnp.float32).astype(jnp.bfloat16),
        "mp",
        scatter_dimension=0,
        tiled=True,
    ).astype(jnp.float32)
    hidden_out = (middle + ffn_out).astype(jnp.bfloat16)
    regathered = (
        lax.all_gather(attn_in, "dp", axis=0, tiled=True),
        lax.all_gather(attn_out, "dp", axis=1, tiled=True),
        lax.all_gather(w_gate, "dp", axis=0, tiled=True),
        lax.all_gather(w_up, "dp", axis=0, tiled=True),
        lax.all_gather(w_down, "dp", axis=1, tiled=True),
        lax.all_gather(norm1_gain, "dp", axis=0, tiled=True),
        lax.all_gather(norm2_gain, "dp", axis=0, tiled=True),
    )
    qkv_weight, out_weight = (
        lax.all_gather(regathered[0], "mp", axis=1, tiled=True),
        lax.all_gather(regathered[1], "mp", axis=0, tiled=True),
    )
    gate_weight, up_weight, down_weight = (regathered[2], regathered[3], regathered[4])
    gain_one = regathered[5].astype(jnp.float32)
    gain_two = regathered[6].astype(jnp.float32)
    cot_local = cotangent[0]
    seq_cot = lax.all_gather(cot_local, "mp", axis=0, tiled=True)
    g_down = jnp.dot(hidden_b.T, seq_cot, preferred_element_type=jnp.float32)
    grad_hid = jnp.dot(seq_cot, down_weight.T, preferred_element_type=jnp.float32)
    grad_gate_act = (grad_hid * upper * sigma * (1.0 + gate * (1.0 - sigma))).astype(jnp.bfloat16)
    grad_up_act = (grad_hid * silu_gate).astype(jnp.bfloat16)
    g_gate = jnp.dot(seq_normed.T, grad_gate_act, preferred_element_type=jnp.float32)
    g_up = jnp.dot(seq_normed.T, grad_up_act, preferred_element_type=jnp.float32)
    grad_norm2 = lax.psum_scatter(
        jnp.dot(grad_gate_act, gate_weight.T, preferred_element_type=jnp.float32)
        + jnp.dot(grad_up_act, up_weight.T, preferred_element_type=jnp.float32),
        "mp",
        scatter_dimension=0,
        tiled=True,
    )
    grad_mid_norm, g_gain2 = rms_backward(middle, inv_two, gain_two, grad_norm2)
    grad_middle = cot_local.astype(jnp.float32) + grad_mid_norm
    middle_b = grad_middle.astype(jnp.bfloat16)
    g_out = jnp.dot(attn_b.T, middle_b, preferred_element_type=jnp.float32)
    grad_attn_b = jnp.dot(middle_b, out_weight.T, preferred_element_type=jnp.float32).astype(
        jnp.bfloat16
    )
    grad_groups = grad_attn_b.reshape(tok_rows, KV_HEADS, group_size, HEAD_DIM).transpose(
        1, 2, 0, 3
    )
    grad_q, grad_k, grad_v = lax.map(
        lambda pack: attend_back(pack[0], pack[1], pack[2], allowed, pack[3], pack[4], pack[5]),
        (query_groups, key_groups, value_groups, log_totals, out_groups, grad_groups),
    )
    key_grads, value_grads = (
        lax.psum_scatter(grad_k, "mp", scatter_dimension=1, tiled=True),
        lax.psum_scatter(grad_v, "mp", scatter_dimension=1, tiled=True),
    )
    grad_q = rotate_back(
        grad_q.transpose(2, 0, 1, 3).reshape(tok_rows, HEADS, HEAD_DIM), cosine, sine
    )
    key_grads = rotate_back(key_grads.transpose(1, 0, 2), cosine, sine)
    value_grads = value_grads.transpose(1, 0, 2)
    grad_proj = jnp.concatenate(
        [
            grad_q.reshape(tok_rows, query_cols),
            key_grads.reshape(tok_rows, kv_cols),
            value_grads.reshape(tok_rows, kv_cols),
        ],
        axis=1,
    ).astype(jnp.bfloat16)
    g_in = jnp.dot(normed1_b.T, grad_proj, preferred_element_type=jnp.float32)
    grad_norm1 = jnp.dot(grad_proj, qkv_weight.T, preferred_element_type=jnp.float32)
    grad_in_norm, g_gain1 = rms_backward(resid_in, inv_one, gain_one, grad_norm1)
    grad_input = grad_middle + grad_in_norm
    reduced = (
        lax.psum_scatter(g_in, "dp", scatter_dimension=0, tiled=True),
        lax.psum_scatter(g_out, "dp", scatter_dimension=1, tiled=True),
        lax.psum_scatter(g_gate, "dp", scatter_dimension=0, tiled=True),
        lax.psum_scatter(g_up, "dp", scatter_dimension=0, tiled=True),
        lax.psum_scatter(g_down, "dp", scatter_dimension=1, tiled=True),
        lax.psum_scatter(g_gain1, "dp", scatter_dimension=0, tiled=True),
        lax.psum_scatter(g_gain2, "dp", scatter_dimension=0, tiled=True),
    )
    grad_attn_in, grad_attn_out = (
        lax.psum_scatter(reduced[0], "mp", scatter_dimension=1, tiled=True),
        lax.psum_scatter(reduced[1], "mp", scatter_dimension=0, tiled=True),
    )
    grad_gain1, grad_gain2 = lax.psum((reduced[5], reduced[6]), "mp")
    return (
        hidden_out[None],
        grad_input[None],
        grad_attn_in,
        grad_attn_out,
        reduced[2],
        reduced[3],
        reduced[4],
        grad_gain1,
        grad_gain2,
    )


def solution(mesh):
    return jax.shard_map(
        per_device,
        mesh=mesh,
        in_specs=(
            P("dp", "mp", None),
            P("dp", "mp", None),
            P("dp", None),
            P("dp", "mp"),
            P("dp", "mp"),
            P("mp", "dp"),
            P("dp", "mp"),
            P("dp", "mp"),
            P("mp", "dp"),
            P("dp"),
            P("dp"),
        ),
        out_specs=(
            P("dp", "mp", None),
            P("dp", "mp", None),
            P("dp", "mp"),
            P("mp", "dp"),
            P("dp", "mp"),
            P("dp", "mp"),
            P("mp", "dp"),
            P("dp"),
            P("dp"),
        ),
        check_vma=False,
    )
```

profile of v0, /device:TPU:0, one launch (start us, length us, event | category | flops | bytes accessed | tf_op | source)
XLA Modules:
  0.0 1195.8 jit_solution(7193035129277229926)
XLA Ops:
  7.3 34.3 %all-gather.1 = bf16[8,120,400]{1,2,0:T(8,128)(2,1)S(1)} all-gather(bf16[1,120,400]{1,2,0:T(8,128)(2,1)} %bitcast.241), channel_id=1, replica_groups=mesh['dp'=8,'mp'=4] {'dp'}, dimensions={0}, use_global_device_ids=true | all-gather | bytes 864000 | tf_op jit(solution)/shard_map/all_gather | solution.py:113
  45.2 21.3 %all-reduce.10 = (bf16[960]{0:T(1024)(128)(2,1)S(1)}, bf16[960]{0:T(1024)(128)(2,1)S(1)}) all-reduce(bf16[960]{0:T(1024)(128)(2,1)S(1)} %dynamic-update-slice, bf16[960]{0:T(1024)(128)(2,1)S(1)} %dynamic-update-slice.1), channel_id=1, replica_groups=mesh['dp'=8,'mp'=4] {'dp'}, use_global_device_ids=true, to_apply=%add | all-reduce | flops 1920 | bytes 7680
  80.2 33.2 %all_gather.53 = bf16[240,960]{0,1:T(8,128)(2,1)} all-gather(bf16[240,120]{0,1:T(8,128)(2,1)S(1)} %copy.27), channel_id=1, replica_groups=mesh['dp'=8,'mp'=4] {'dp'}, dimensions={1}, use_global_device_ids=true | all-gather | bytes 518400 | tf_op jit(solution)/shard_map/all_gather | solution.py:114
  117.5 114.8 %while.30 = (s32[]{:T(128)}, bf16[5,3,512,64]{2,3,1,0:T(8,128)(2,1)S(1)}, f32[5,3,512]{2,1,0:T(4,128)S(1)}, bf16[5,3,512,64]{2,3,1,0:T(8,128)(2,1)S(1)}, bf16[5,...) while((s32[]{:T(128)}, ...), condition=%wide.region_4.5_spmd.clone.clone, body=%wide.region_1.4_spmd.clone.sunk.clone | while | flops 843053568 | bytes 43130984 | solution.py:160
  240.1 30.8 %all-gather.20.cloned.1.call-done = bf16[2048,960]{0,1:T(8,128)(2,1)} async-done(((bf16[512,960]{0,1:T(8,128)(2,1)}), bf16[2048,960]{0,1:T(8,128)(2,1)}) %all-gather.20.cloned.1.call-update) | async-done | bytes 3932176 | tf_op jit(solution)/shard_map/all_gather | solution.py:169
  270.9 8.3 fusion.89
  279.2 35.4 %all-gather.22.cloned.1.call-done = bf16[960,640]{1,0:T(8,128)(2,1)} async-done(((bf16[120,640]{1,0:T(8,128)(2,1)}), bf16[960,640]{1,0:T(8,128)(2,1)}) %all-gather.22.cloned.1.call-update) | async-done | bytes 1228816 | tf_op jit(solution)/shard_map/all_gather | solution.py:115
  314.6 8.3 fusion.88
  322.9 34.1 %all-gather.26.cloned.1.call-done = bf16[640,960]{0,1:T(8,128)(2,1)} async-done(((bf16[640,120]{0,1:T(8,128)(2,1)}), bf16[640,960]{0,1:T(8,128)(2,1)}) %all-gather.26.cloned.1.call-update) | async-done | bytes 1228816 | tf_op jit(solution)/shard_map/all_gather | solution.py:117
  357.0 33.4 %all-gather.28.cloned.1.call-done = bf16[1,2048,960]{1,2,0:T(8,128)(2,1)} async-done(((bf16[1,512,960]{1,2,0:T(8,128)(2,1)}), bf16[1,2048,960]{1,2,0:T(8,128)(2,1)}) %all-gather.28.cloned.1.call-update) | async-done | bytes 3932176 | tf_op jit(solution)/shard_map/all_gather | solution.py:199
  390.4 12.7 %multiply_convert_fusion.1 = (bf16[2048,640]{1,0:T(8,128)(2,1)S(1)}, bf16[2048,640]{1,0:T(8,128)(2,1)S(1)}, bf16[2048,640]{1,0:T(8,128)(2,1)}) fusion(f32[2048,640]{1,0:T(8,128)} %fusion.88, f32[2048,640]{1,0:T(8,128)} %fusion.89, bf16[640,960]{0,1:T(8,128)(2,1)} %all-gather.26.cloned.1.call-done, bf16[1,2048,960]{1,2,0:T(8,128)(2,1)} %all-gather.28.cloned.1.call-done), kind=kOutput, calls=%fused_computation.66 | convolution fusion | flops 2536243200 | bytes 23511040 | tf_op jit(solution)/shard_map/dot_general | solution.py:201
  419.3 61.8 %reduce-scatter.26.cloned.1.call-done = f32[512,960]{0,1:T(8,128)} async-done(((f32[2048,960]{0,1:T(8,128)}), f32[512,960]{0,1:T(8,128)}) %reduce-scatter.26.cloned.1.call-update) | async-done | bytes 1966096 | tf_op jit(solution)/shard_map/reduce_scatter | solution.py:206
  483.8 42.9 %reduce-scatter.24.cloned.1.call-done = bf16[512,960]{0,1:T(8,128)(2,1)} async-done(((bf16[2048,960]{0,1:T(8,128)(2,1)}), bf16[512,960]{0,1:T(8,128)(2,1)}) %reduce-scatter.24.cloned.1.call-update) | async-done | bytes 983056 | tf_op jit(solution)/shard_map/reduce_scatter | solution.py:175
  531.9 101.6 %while.31 = (s32[]{:T(128)}, f32[5,3,512,64]{2,3,1,0:T(8,128)}, f32[5,2048,64]{1,2,0:T(8,128)}, f32[5,2048,64]{1,2,0:T(8,128)}, bf16[5,3,512,64]{2,3,1,0:T(8,128...) while((s32[]{:T(128)}, f32[5,3,512,64]{2,3,1,0:T(8,128)}, ...), condition=%wide.region_11.12_spmd.clone.clone, body=%wide.region_9.11_spmd.clone.sunk.clone | while | flops 2048489984 | bytes 63237260 | solution.py:223
  641.9 26.4 %reduce-scatter.30.cloned.1.call-done = f32[5,512,64]{1,2,0:T(8,128)} async-done(((f32[5,2048,64]{1,2,0:T(8,128)}), f32[5,512,64]{1,2,0:T(8,128)}) %reduce-scatter.30.cloned.1.call-update) | async-done | bytes 655376 | tf_op jit(solution)/shard_map/reduce_scatter | solution.py:229
  670.2 35.5 %reduce-scatter.28.cloned.1.call-done = f32[5,512,64]{1,2,0:T(8,128)} async-done(((f32[5,2048,64]{1,2,0:T(8,128)}), f32[5,512,64]{1,2,0:T(8,128)}) %reduce-scatter.28.cloned.1.call-update) | async-done | bytes 655376 | tf_op jit(solution)/shard_map/reduce_scatter | solution.py:228
  736.1 57.5 %reduce-scatter.36.cloned.1.call-done = f32[120,960]{1,0:T(8,128)} async-done(((f32[960,960]{1,0:T(8,128)}), f32[120,960]{1,0:T(8,128)}) %reduce-scatter.36.cloned.1.call-update) | async-done | bytes 460816
  796.0 122.4 %reduce-scatter.38.cloned.1.call-done = f32[120,1600]{1,0:T(8,128)} async-done(((f32[960,1600]{1,0:T(8,128)}), f32[120,1600]{1,0:T(8,128)}) %reduce-scatter.38.cloned.1.call-update) | async-done | bytes 768016
  927.2 20.1 %all-reduce.8 = (f32[960]{0:T(1024)S(1)}, f32[960]{0:T(1024)S(1)}) all-reduce(f32[960]{0:T(1024)S(1)} %get-tuple-element.203, f32[960]{0:T(1024)S(1)} %copy-done.14), channel_id=14, replica_groups=mesh['dp'=8,'mp'=4] {'dp'}, use_global_device_ids=true, to_apply=%region_23.24.clone | all-reduce | flops 1920 | bytes 15360
  957.3 34.7 %reduce-scatter.44.cloned.1.call-done = f32[640,120]{0,1:T(8,128)} async-done(((f32[640,960]{0,1:T(8,128)}), f32[640,120]{0,1:T(8,128)}) %reduce-scatter.44.cloned.1.call-update) | async-done | bytes 307216
  992.0 73.3 %reduce-scatter.40.cloned.1.call-done = f32[120,640]{1,0:T(8,128)} async-done(((f32[960,640]{1,0:T(8,128)}), f32[120,640]{1,0:T(8,128)}) %reduce-scatter.40.cloned.1.call-update) | async-done | bytes 307216
  1065.3 73.2 %reduce-scatter.42.cloned.1.call-done = f32[120,640]{1,0:T(8,128)} async-done(((f32[960,640]{1,0:T(8,128)}), f32[120,640]{1,0:T(8,128)}) %reduce-scatter.42.cloned.1.call-update) | async-done | bytes 307216
  1138.5 23.6 %reduce-scatter.32.cloned.1.call-done = f32[240,120]{1,0:T(8,128)} async-done(((f32[960,120]{1,0:T(8,128)}), f32[240,120]{1,0:T(8,128)}) %reduce-scatter.32.cloned.1.call-update) | async-done | bytes 115216 | tf_op jit(solution)/shard_map/reduce_scatter | solution.py:259
  1162.1 26.6 %reduce-scatter.34.cloned.1.call-done = f32[400,120]{1,0:T(8,128)} async-done(((f32[1600,120]{1,0:T(8,128)}), f32[400,120]{1,0:T(8,128)}) %reduce-scatter.34.cloned.1.call-update) | async-done | bytes 192016
  (222 shorter events, 329.0 us)
Async XLA Ops:
  7.2 59.3 %copy-start.5 = (bf16[1,512,960]{1,2,0:T(8,128)(2,1)S(1)}, bf16[1,512,960]{1,2,0:T(8,128)(2,1)}, u32[]{:S(2)}) copy-start(bf16[1,512,960]{1,2,0:T(8,128)(2,1)} %param.15) | copy-start | bytes 2949124
  7.2 66.5 %all-gather.12.cloned.1.call-start = ((), (), s32[]{:S(2)}) async-start(), calls=%async_computation.11 | async-start | bytes 4096000 | tf_op jit(solution)/shard_map/all_gather | solution.py:122
  43.4 74.1 %all-gather.16.cloned.1.call-start = ((), (), s32[]{:S(2)}) async-start(), calls=%async_computation.13 | async-start | bytes 1638400 | tf_op jit(solution)/shard_map/all_gather | solution.py:148
  78.7 38.8 %all-gather.14.cloned.1.call-start = ((), (), s32[]{:S(2)}) async-start(), calls=%async_computation.12 | async-start | bytes 1638400 | tf_op jit(solution)/shard_map/all_gather | solution.py:147
  80.1 152.3 %all-gather.18.cloned.1.call-start = ((), (), s32[]{:S(2)}) async-start(), calls=%async_computation.14 | async-start | bytes 2457600 | tf_op jit(solution)/shard_map/all_gather | solution.py:123
  115.5 124.6 %all-gather.24.cloned.1.call-start = ((), (), s32[]{:S(2)}) async-start(), calls=%async_computation.17 | async-start | bytes 1382400 | tf_op jit(solution)/shard_map/all_gather | solution.py:116
  116.1 154.8 %all-gather.20.cloned.1.call-start = ((), (), s32[]{:S(2)}) async-start(), calls=%async_computation.15 | async-start | bytes 4915200 | tf_op jit(solution)/shard_map/all_gather | solution.py:169
  237.5 77.0 %all-gather.22.cloned.1.call-start = ((), (), s32[]{:S(2)}) async-start(), calls=%async_computation.16 | async-start | bytes 1382400 | tf_op jit(solution)/shard_map/all_gather | solution.py:115
  238.3 118.7 %all-gather.26.cloned.1.call-start = ((), (), s32[]{:S(2)}) async-start(), calls=%async_computation.18 | async-start | bytes 1382400 | tf_op jit(solution)/shard_map/all_gather | solution.py:117
  239.1 151.4 %all-gather.28.cloned.1.call-start = ((), (), s32[]{:S(2)}) async-start(), calls=%async_computation.24 | async-start | bytes 4915200 | tf_op jit(solution)/shard_map/all_gather | solution.py:199
  239.8 241.3 %reduce-scatter.26.cloned.1.call-start = ((), (), s32[]{:S(2)}) async-start(), calls=%async_computation.20 | async-start | bytes 9830400 | tf_op jit(solution)/shard_map/reduce_scatter | solution.py:206
  412.0 114.8 %reduce-scatter.24.cloned.1.call-start = ((), (), s32[]{:S(2)}) async-start(), calls=%async_computation.19 | async-start | bytes 4915200 | tf_op jit(solution)/shard_map/reduce_scatter | solution.py:175
  419.2 249.1 %reduce-scatter.30.cloned.1.call-start = ((), (), s32[]{:S(2)}) async-start(), calls=%async_computation.22 | async-start | bytes 3276800 | tf_op jit(solution)/shard_map/reduce_scatter | solution.py:229
  633.5 72.2 %reduce-scatter.28.cloned.1.call-start = ((), (), s32[]{:S(2)}) async-start(), calls=%async_computation.21 | async-start | bytes 3276800 | tf_op jit(solution)/shard_map/reduce_scatter | solution.py:228
  634.2 159.4 %reduce-scatter.36.cloned.1.call-start = ((), (), s32[]{:S(2)}) async-start(), calls=%async_computation.26 | async-start | bytes 4423680
  638.2 280.3 %reduce-scatter.38.cloned.1.call-start = ((), (), s32[]{:S(2)}) async-start(), calls=%async_computation.27 | async-start | bytes 7188480
  640.9 66.1 %copy-start.6 = (bf16[1,512,960]{1,2,0:T(8,128)(2,1)S(1)}, bf16[1,512,960]{1,2,0:T(8,128)(2,1)}, u32[]{:S(2)}) copy-start(bf16[1,512,960]{1,2,0:T(8,128)(2,1)} %param.15) | copy-start | bytes 2949124
  640.9 66.1 %copy-start.16 = (f32[960]{0:T(1024)S(1)}, f32[960]{0:T(1024)}, u32[]{:S(2)}) copy-start(f32[960]{0:T(1024)} %copy-done.15) | copy-start | bytes 11524
  640.9 66.1 %copy-start.18 = (f32[512]{0:T(512)S(1)}, f32[512]{0:T(512)}, u32[]{:S(2)}) copy-start(f32[512]{0:T(512)} %copy-done.17) | copy-start | bytes 6148
  713.0 279.0 %reduce-scatter.44.cloned.1.call-start = ((), (), s32[]{:S(2)}) async-start(), calls=%async_computation.30 | async-start | bytes 2764800
  720.6 344.7 %reduce-scatter.40.cloned.1.call-start = ((), (), s32[]{:S(2)}) async-start(), calls=%async_computation.28 | async-start | bytes 2764800
  728.3 410.2 %reduce-scatter.42.cloned.1.call-start = ((), (), s32[]{:S(2)}) async-start(), calls=%async_computation.29 | async-start | bytes 2764800
  736.0 426.0 %reduce-scatter.32.cloned.1.call-start = ((), (), s32[]{:S(2)}) async-start(), calls=%async_computation.23 | async-start | bytes 614400 | tf_op jit(solution)/shard_map/reduce_scatter | solution.py:259
  795.7 393.0 %reduce-scatter.34.cloned.1.call-start = ((), (), s32[]{:S(2)}) async-start(), calls=%async_computation.25 | async-start | bytes 1024000
  (23 other events, 337.1 us)
Sparse Core Ops, SparseCore 0:
  43.5 30.1 all-gather.11
  78.8 18.1 all-gather.15
  99.2 18.1 all-gather.13
  119.4 21.8 all-gather.17
  143.3 41.4 all-gather.23
  237.7 33.2 all-gather.19
  273.1 41.4 all-gather.21
  316.8 40.2 all-gather.25
  358.6 31.7 all-gather.27
  412.1 68.9 reduce-scatter.25
  483.8 42.8 reduce-scatter.23
  633.6 34.6 reduce-scatter.29
  671.0 34.6 reduce-scatter.27
  709.3 84.3 reduce-scatter.35
  797.5 120.8 reduce-scatter.37
  922.9 69.0 reduce-scatter.43
  996.5 68.8 reduce-scatter.39
  1069.8 68.6 reduce-scatter.41
  1141.7 20.2 reduce-scatter.31
  1165.2 23.4 reduce-scatter.33
where the time goes:
time: 1200 us
  waiting for transfers between devices  722 us (60%)
  matrix products  261 us (22%)
  blocking collectives  115 us (10%)
  other arithmetic  65.6 us (5%)
  between operations  16.4 us (1%)
  local copies, waits for them, and re-layouts  13.4 us (1%)
    unnamed x26, waiting for transfers between devices  391 us
    reduce_scatter x1, waiting for transfers between devices, per_device(): lax.psum_scatter(jnp.dot(grad_gate_act, gate_weight.T, preferred_element_...  61.8 us
    dot_general x10, matrix products, score_block(): jnp.einsum('grd,sd->grs', queries, keys, preferred_element_type=jnp.float32)  48.5 us
    reduce_scatter x1, waiting for transfers between devices, per_device(): lax.psum_scatter(jnp.dot(hidden_b, down_weight, preferred_element_type=jn...  42.9 us
    unnamed x2, blocking collectives  41.4 us
    dot_general x5, matrix products, attend(): jnp.einsum('grs,sd->grd', probs, values, preferred_element_type=jnp.float32)  40.2 us
    reduce_scatter x1, waiting for transfers between devices, per_device(): lax.psum_scatter(grad_k, 'mp', scatter_dimension=1, tiled=True)  35.5 us
    all_gather x1, waiting for transfers between devices, per_device(): lax.all_gather(w_gate, 'dp', axis=0, tiled=True)  35.4 us
  transfers between devices with their start and end apart: 20, of which 16 were waited for; matrix products, arithmetic and copies ran while one was open for 17% of the time, Pallas kernels for 0%

commit v1 on v0

--- a/solution.py
+++ b/solution.py
@@ -10,6 +10,27 @@
 EPSILON = 1e-05
 SCORE_SCALE = 0.125
 MASK_FILL = -1e30
+
+
+def gather_around(x, axis, dim):
+    peers, index, width = (lax.axis_size(axis), lax.axis_index(axis), x.shape[dim])
+    right = [(i, (i + 1) % peers) for i in range(peers)]
+    left = [(i, (i - 1) % peers) for i in range(peers)]
+    result = jnp.zeros((*x.shape[:dim], peers * width, *x.shape[dim + 1 :]), x.dtype)
+    result = lax.dynamic_update_slice_in_dim(result, x, index * width, axis=dim)
+    from_left = from_right = x
+    halfway = peers // 2
+    for step in range(1, halfway + 1):
+        from_left = lax.ppermute(from_left, axis, right)
+        result = lax.dynamic_update_slice_in_dim(
+            result, from_left, (index - step) % peers * width, axis=dim
+        )
+        if step < peers - halfway:
+            from_right = lax.ppermute(from_right, axis, left)
+            result = lax.dynamic_update_slice_in_dim(
+                result, from_right, (index + step) % peers * width, axis=dim
+            )
+    return result
 
 
 def rms_forward(values_in, gain):
@@ -112,7 +133,7 @@
     gathered = (
         lax.all_gather(attn_in, "dp", axis=0, tiled=True),
         lax.all_gather(attn_out, "dp", axis=1, tiled=True),
-        lax.all_gather(w_gate, "dp", axis=0, tiled=True),
+        gather_around(w_gate, "dp", 0),
         lax.all_gather(w_up, "dp", axis=0, tiled=True),
         lax.all_gather(w_down, "dp", axis=1, tiled=True),
         lax.all_gather(norm1_gain, "dp", axis=0, tiled=True),

time: 1200 us -> 1150 us (0.958)
  waiting for transfers between devices: 722 us -> 649 us
  starting transfers between devices: 1.66 us -> 17.2 us
    all_gather x1, waiting for transfers between devices: 34.1 us -> 0.01 us  [per_device(): lax.all_gather(w_down, 'dp', axis=1, tiled=True)]
    all_gather x1, waiting for transfers between devices: 33.4 us -> 0.01 us  [per_device(): seq_cot = lax.all_gather(cot_local, 'mp', axis=0, tiled=True)]
    ppermute x0 -> x7, starting transfers between devices: none -> 15.8 us  [the longest x3 8.47 us: gather_around(): from_right = lax.ppermute(from_right, axis, left)]
    ppermute x0 -> x7, waiting for transfers between devices: none -> 14.1 us  [the longest x4 13.2 us: gather_around(): from_left = lax.ppermute(from_left, axis, right)]
  transfers between devices with their start and end apart: 20 -> 27, of which waited for: 16 -> 21; matrix products, arithmetic and copies ran while one was open for 17% -> 19% of each run, Pallas kernels for 0% -> 0%
where the time goes in v1:
time: 1150 us; the launch traced here: 1140 us
  waiting for transfers between devices  649 us (56%)
  matrix products  258 us (22%)
  blocking collectives  114 us (10%)
  other arithmetic  65.6 us (6%)
  local copies, waits for them, and re-layouts  23.3 us (2%)
  starting transfers between devices  17.2 us (1%)
  between operations  16.6 us (1%)
    unnamed x26, waiting for transfers between devices  390 us
    reduce_scatter x1, waiting for transfers between devices, per_device(): lax.psum_scatter(jnp.dot(grad_gate_act, gate_weight.T, preferred_element_...  60.6 us
    dot_general x10, matrix products, score_block(): jnp.einsum('grd,sd->grs', queries, keys, preferred_element_type=jnp.float32)  49.4 us
    reduce_scatter x1, waiting for transfers between devices, per_device(): lax.psum_scatter(jnp.dot(hidden_b, down_weight, preferred_element_type=jn...  42.9 us
    unnamed x2, blocking collectives  41.4 us
    dot_general x5, matrix products, attend(): jnp.einsum('grs,sd->grd', probs, values, preferred_element_type=jnp.float32)  40.4 us
    reduce_scatter x1, waiting for transfers between devices, per_device(): lax.psum_scatter(grad_k, 'mp', scatter_dimension=1, tiled=True)  35.6 us
    reduce_sum x5, other arithmetic, attend(): total = jnp.sum(jnp.exp(scores - peak), axis=-1, keepdims=True)  34.3 us
  transfers between devices with their start and end apart: 27, of which 21 were waited for; matrix products, arithmetic and copies ran while one was open for 19% of the time, Pallas kernels for 0%

profile of v1, /device:TPU:0, one launch (start us, length us, event | category | flops | bytes accessed | tf_op | source)
XLA Modules:
  0.0 1144.1 jit_solution(14545484000678571474)
XLA Ops:
  7.3 34.3 %all-gather.1 = bf16[8,120,400]{1,2,0:T(8,128)(2,1)S(1)} all-gather(bf16[1,120,400]{1,2,0:T(8,128)(2,1)} %bitcast.239), channel_id=1, replica_groups=mesh['dp'=8,'mp'=4] {'dp'}, dimensions={0}, use_global_device_ids=true | all-gather | bytes 864000 | tf_op jit(solution)/shard_map/all_gather | solution.py:134
  45.2 21.3 %all-reduce.10 = (bf16[960]{0:T(1024)(128)(2,1)S(1)}, bf16[960]{0:T(1024)(128)(2,1)S(1)}) all-reduce(bf16[960]{0:T(1024)(128)(2,1)S(1)} %dynamic-update-slice, bf16[960]{0:T(1024)(128)(2,1)S(1)} %dynamic-update-slice.1), channel_id=1, replica_groups=mesh['dp'=8,'mp'=4] {'dp'}, use_global_device_ids=true, to_apply=%add | all-reduce | flops 1920 | bytes 7680
  82.8 31.5 %all_gather.52 = bf16[240,960]{0,1:T(8,128)(2,1)S(1)} all-gather(bf16[240,120]{0,1:T(8,128)(2,1)S(1)} %copy.27), channel_id=1, replica_groups=mesh['dp'=8,'mp'=4] {'dp'}, dimensions={1}, use_global_device_ids=true | all-gather | bytes 518400 | tf_op jit(solution)/shard_map/all_gather | solution.py:135
  118.8 115.9 %while.30 = (s32[]{:T(128)}, bf16[5,3,512,64]{2,3,1,0:T(8,128)(2,1)S(1)}, f32[5,3,512]{2,1,0:T(4,128)S(1)}, bf16[5,3,512,64]{2,3,1,0:T(8,128)(2,1)S(1)}, bf16[5,...) while((s32[]{:T(128)}, ...), condition=%wide.region_4.5_spmd.clone.clone, body=%wide.region_1.4_spmd.clone.sunk.clone | while | flops 843053568 | bytes 43130984 | solution.py:181
  134.1 8.1 fusion.159
  203.6 8.1 fusion.159
  226.5 8.2 fusion.159
  278.5 8.7 fusion.63
  287.2 19.4 %all-gather.20.cloned.1.call-done = bf16[2048,960]{0,1:T(8,128)(2,1)} async-done(((bf16[512,960]{0,1:T(8,128)(2,1)}), bf16[2048,960]{0,1:T(8,128)(2,1)}) %all-gather.20.cloned.1.call-update) | async-done | bytes 3932176 | tf_op jit(solution)/shard_map/all_gather | solution.py:190
  312.8 9.1 multiply_convert_fusion.1
  321.8 28.5 %all-gather.26.cloned.1.call-done = bf16[960,640]{1,0:T(8,128)(2,1)} async-done(((bf16[120,640]{1,0:T(8,128)(2,1)}), bf16[960,640]{1,0:T(8,128)(2,1)}) %all-gather.26.cloned.1.call-update) | async-done | bytes 1228816 | tf_op jit(solution)/shard_map/all_gather | solution.py:206
  368.7 60.6 %reduce-scatter.26.cloned.1.call-done = f32[512,960]{0,1:T(8,128)} async-done(((f32[2048,960]{0,1:T(8,128)}), f32[512,960]{0,1:T(8,128)}) %reduce-scatter.26.cloned.1.call-update) | async-done | bytes 1966096 | tf_op jit(solution)/shard_map/reduce_scatter | solution.py:227
  432.0 42.9 %reduce-scatter.24.cloned.1.call-done = bf16[512,960]{0,1:T(8,128)(2,1)} async-done(((bf16[2048,960]{0,1:T(8,128)(2,1)}), bf16[512,960]{0,1:T(8,128)(2,1)}) %reduce-scatter.24.cloned.1.call-update) | async-done | bytes 983056 | tf_op jit(solution)/shard_map/reduce_scatter | solution.py:196
  480.0 101.7 %while.31 = (s32[]{:T(128)}, f32[5,3,512,64]{2,3,1,0:T(8,128)}, f32[5,2048,64]{1,2,0:T(8,128)}, f32[5,2048,64]{1,2,0:T(8,128)}, bf16[5,3,512,64]{2,3,1,0:T(8,128...) while((s32[]{:T(128)}, f32[5,3,512,64]{2,3,1,0:T(8,128)}, ...), condition=%wide.region_11.12_spmd.clone.clone, body=%wide.region_9.11_spmd.clone.sunk.clone | while | flops 2048489984 | bytes 63237260 | solution.py:244
  590.1 26.4 %reduce-scatter.30.cloned.1.call-done = f32[5,512,64]{1,2,0:T(8,128)} async-done(((f32[5,2048,64]{1,2,0:T(8,128)}), f32[5,512,64]{1,2,0:T(8,128)}) %reduce-scatter.30.cloned.1.call-update) | async-done | bytes 655376 | tf_op jit(solution)/shard_map/reduce_scatter | solution.py:250
  618.4 35.6 %reduce-scatter.28.cloned.1.call-done = f32[5,512,64]{1,2,0:T(8,128)} async-done(((f32[5,2048,64]{1,2,0:T(8,128)}), f32[5,512,64]{1,2,0:T(8,128)}) %reduce-scatter.28.cloned.1.call-update) | async-done | bytes 655376 | tf_op jit(solution)/shard_map/reduce_scatter | solution.py:249
  684.3 57.6 %reduce-scatter.36.cloned.1.call-done = f32[120,960]{1,0:T(8,128)} async-done(((f32[960,960]{1,0:T(8,128)}), f32[120,960]{1,0:T(8,128)}) %reduce-scatter.36.cloned.1.call-update) | async-done | bytes 460816
  744.3 122.4 %reduce-scatter.38.cloned.1.call-done = f32[120,1600]{1,0:T(8,128)} async-done(((f32[960,1600]{1,0:T(8,128)}), f32[120,1600]{1,0:T(8,128)}) %reduce-scatter.38.cloned.1.call-update) | async-done | bytes 768016
  875.4 20.1 %all-reduce.8 = (f32[960]{0:T(1024)S(1)}, f32[960]{0:T(1024)S(1)}) all-reduce(f32[960]{0:T(1024)S(1)} %get-tuple-element.203, f32[960]{0:T(1024)S(1)} %copy-done.16), channel_id=14, replica_groups=mesh['dp'=8,'mp'=4] {'dp'}, use_global_device_ids=true, to_apply=%region_23.24.clone | all-reduce | flops 1920 | bytes 15360
  905.6 34.8 %reduce-scatter.44.cloned.1.call-done = f32[640,120]{0,1:T(8,128)} async-done(((f32[640,960]{0,1:T(8,128)}), f32[640,120]{0,1:T(8,128)}) %reduce-scatter.44.cloned.1.call-update) | async-done | bytes 307216
  940.4 73.2 %reduce-scatter.40.cloned.1.call-done = f32[120,640]{1,0:T(8,128)} async-done(((f32[960,640]{1,0:T(8,128)}), f32[120,640]{1,0:T(8,128)}) %reduce-scatter.40.cloned.1.call-update) | async-done | bytes 307216
  1013.6 73.1 %reduce-scatter.42.cloned.1.call-done = f32[120,640]{1,0:T(8,128)} async-done(((f32[960,640]{1,0:T(8,128)}), f32[120,640]{1,0:T(8,128)}) %reduce-scatter.42.cloned.1.call-update) | async-done | bytes 307216
  1086.8 23.6 %reduce-scatter.32.cloned.1.call-done = f32[240,120]{1,0:T(8,128)} async-done(((f32[960,120]{1,0:T(8,128)}), f32[240,120]{1,0:T(8,128)}) %reduce-scatter.32.cloned.1.call-update) | async-done | bytes 115216 | tf_op jit(solution)/shard_map/reduce_scatter | solution.py:280
  1110.3 26.6 %reduce-scatter.34.cloned.1.call-done = f32[400,120]{1,0:T(8,128)} async-done(((f32[1600,120]{1,0:T(8,128)}), f32[400,120]{1,0:T(8,128)}) %reduce-scatter.34.cloned.1.call-update) | async-done | bytes 192016
  (249 shorter events, 353.1 us)
Async XLA Ops:
  7.2 66.5 %all-gather.12.cloned.1.call-start = ((), (), s32[]{:S(2)}) async-start(), calls=%async_computation.11 | async-start | bytes 4096000 | tf_op jit(solution)/shard_map/all_gather | solution.py:143
  43.4 75.0 %all-gather.16.cloned.1.call-start = ((), (), s32[]{:S(2)}) async-start(), calls=%async_computation.13 | async-start | bytes 1638400 | tf_op jit(solution)/shard_map/all_gather | solution.py:169
  80.1 38.7 %all-gather.14.cloned.1.call-start = ((), (), s32[]{:S(2)}) async-start(), calls=%async_computation.12 | async-start | bytes 1638400 | tf_op jit(solution)/shard_map/all_gather | solution.py:168
  82.6 152.2 %all-gather.18.cloned.1.call-start = ((), (), s32[]{:S(2)}) async-start(), calls=%async_computation.14 | async-start | bytes 2457600 | tf_op jit(solution)/shard_map/all_gather | solution.py:144
  115.2 163.3 %all-gather.24.cloned.1.call-start = ((), (), s32[]{:S(2)}) async-start(), calls=%async_computation.17 | async-start | bytes 1382400 | tf_op jit(solution)/shard_map/all_gather | solution.py:138
  115.8 162.7 %all-gather.28.cloned.1.call-start = ((), (), s32[]{:S(2)}) async-start(), calls=%async_computation.24 | async-start | bytes 4915200 | tf_op jit(solution)/shard_map/all_gather | solution.py:220
  116.4 170.8 %all-gather.22.cloned.1.call-start = ((), (), s32[]{:S(2)}) async-start(), calls=%async_computation.16 | async-start | bytes 1382400 | tf_op jit(solution)/shard_map/all_gather | solution.py:137
  117.2 189.5 %all-gather.20.cloned.1.call-start = ((), (), s32[]{:S(2)}) async-start(), calls=%async_computation.15 | async-start | bytes 4915200 | tf_op jit(solution)/shard_map/all_gather | solution.py:190
  240.0 110.3 %all-gather.26.cloned.1.call-start = ((), (), s32[]{:S(2)}) async-start(), calls=%async_computation.19 | async-start | bytes 1382400 | tf_op jit(solution)/shard_map/all_gather | solution.py:206
  240.0 10.0 collective-permute-start
  241.5 11.7 %collective-permute-start.1 = (bf16[120,640]{1,0:T(8,128)(2,1)S(1)}, bf16[120,640]{1,0:T(8,128)(2,1)}, u32[]{:S(2)}, u32[]{:S(2)}) collective-permute-start(bf16[120,640]{1,0:T(8,128)(2,1)S(1)} %copy-done.13), channel_id=1, source_target_pairs={{0,28},{4,0},{8,4},{12,8},{16,12},{20,16},{24,20},{28,24},{1,29},{... | collective-permute-start | bytes 460808 | tf_op jit(solution)/shard_map/ppermute | solution.py:29
  244.8 184.5 %reduce-scatter.26.cloned.1.call-start = ((), (), s32[]{:S(2)}) async-start(), calls=%async_computation.20 | async-start | bytes 9830400 | tf_op jit(solution)/shard_map/reduce_scatter | solution.py:227
  250.0 11.6 %collective-permute-start.2 = (bf16[120,640]{1,0:T(8,128)(2,1)}, bf16[120,640]{1,0:T(8,128)(2,1)S(1)}, u32[]{:S(2)}, u32[]{:S(2)}) collective-permute-start(bf16[120,640]{1,0:T(8,128)(2,1)} %collective-permute-done), channel_id=1, source_target_pairs={{0,4},{4,8},{8,12},{12,16},{16,20},{20,24},{24,28},{28,0},{1,5},{5... | collective-permute-start | bytes 460808 | tf_op jit(solution)/shard_map/ppermute | solution.py:24
  253.2 10.9 collective-permute-start.3
  361.3 113.5 %reduce-scatter.24.cloned.1.call-start = ((), (), s32[]{:S(2)}) async-start(), calls=%async_computation.18 | async-start | bytes 4915200 | tf_op jit(solution)/shard_map/reduce_scatter | solution.py:196
  368.6 247.9 %reduce-scatter.30.cloned.1.call-start = ((), (), s32[]{:S(2)}) async-start(), calls=%async_computation.22 | async-start | bytes 3276800 | tf_op jit(solution)/shard_map/reduce_scatter | solution.py:250
  581.7 72.2 %reduce-scatter.28.cloned.1.call-start = ((), (), s32[]{:S(2)}) async-start(), calls=%async_computation.21 | async-start | bytes 3276800 | tf_op jit(solution)/shard_map/reduce_scatter | solution.py:249
  582.5 159.4 %reduce-scatter.36.cloned.1.call-start = ((), (), s32[]{:S(2)}) async-start(), calls=%async_computation.26 | async-start | bytes 4423680
  586.3 280.3 %reduce-scatter.38.cloned.1.call-start = ((), (), s32[]{:S(2)}) async-start(), calls=%async_computation.27 | async-start | bytes 7188480
  661.2 279.2 %reduce-scatter.44.cloned.1.call-start = ((), (), s32[]{:S(2)}) async-start(), calls=%async_computation.30 | async-start | bytes 2764800
  668.8 344.8 %reduce-scatter.40.cloned.1.call-start = ((), (), s32[]{:S(2)}) async-start(), calls=%async_computation.28 | async-start | bytes 2764800
  676.6 410.2 %reduce-scatter.42.cloned.1.call-start = ((), (), s32[]{:S(2)}) async-start(), calls=%async_computation.29 | async-start | bytes 2764800
  684.2 426.1 %reduce-scatter.32.cloned.1.call-start = ((), (), s32[]{:S(2)}) async-start(), calls=%async_computation.23 | async-start | bytes 614400 | tf_op jit(solution)/shard_map/reduce_scatter | solution.py:280
  744.0 393.0 %reduce-scatter.34.cloned.1.call-start = ((), (), s32[]{:S(2)}) async-start(), calls=%async_computation.25 | async-start | bytes 1024000
  (32 other events, 583.8 us)
Sparse Core Ops, SparseCore 0:
  43.5 30.1 all-gather.11
  80.2 18.1 all-gather.15
  100.6 18.1 all-gather.13
  120.8 21.8 all-gather.17
  144.7 41.4 all-gather.23
  187.6 31.7 all-gather.27
  221.6 49.8 all-gather.21
  273.6 32.9 all-gather.19
  308.8 41.4 all-gather.25
  361.5 67.7 reduce-scatter.25
  432.0 42.8 reduce-scatter.23
  581.8 34.6 reduce-scatter.29
  619.2 34.6 reduce-scatter.27
  657.5 84.3 reduce-scatter.35
  745.8 120.7 reduce-scatter.37
  871.1 69.2 reduce-scatter.43
  944.9 68.7 reduce-scatter.39
  1018.1 68.6 reduce-scatter.41
  1090.0 20.2 reduce-scatter.31
  1113.5 23.4 reduce-scatter.33
